TPU v7x, 256 devices: a whole 4x4x8 slice. The times are simulated.
256 devices in a mesh: dp: 32 (over x, y, core), tensor: 8 (over z).
Axes of the slice: x: 4, y: 4, z: 8, core: 2. Of those that a mesh axis runs over, the one named last changes fastest.
Arguments:
- output_gradient: bfloat16 [8192, 8192], P('dp', 'tensor'), may hold values from -96 to 96
- hidden: bfloat16 [8192, 28672], P('dp', 'tensor'), may hold values from -3 to 3
- adapter_down: bfloat16 [64, 16, 28672], P('dp', None, 'tensor'), may hold values from -0.03125 to 0.03125
- adapter_up: bfloat16 [64, 16, 8192], P('dp', None, 'tensor'), may hold values from -0.0625 to 0.0625
- counts: int32 [64], replicated, may hold values from 32 to 288, as said below
- offsets: int32 [64], replicated, may hold values from 0 to 8160, as said below
- adapter_slot: int32 [64], replicated, may hold values from 0 to 63, as said below
Outputs:
- adapter_hidden_gradient: bfloat16 [8192, 28672], P('dp', 'tensor')
- adapter_down_gradient: float32 [64, 16, 28672], P('dp', None, 'tensor')
- adapter_up_gradient: float32 [64, 16, 8192], P('dp', None, 'tensor')
Inputs may be any that keep to these rules, and one draw needn't show every extreme that they name: counts sum to 8192; the last adapter has exactly 32 tokens; exactly one adapter has 288 tokens, every other fewer. Tokens are grouped by adapter in increasing order: offsets[a] is the sum of counts of the adapters before a. `adapter_slot`: every slot holds exactly one adapter; slot k lies on dp index k // 2, and any 64 // 2 adapters in a row lie on distinct dp indices.
All inputs are finite; a program needn't handle non-finite values.
Results may differ from a plain program's by a relative error of at most 0.0075.
Values may be sent and summed in bfloat16 or wider, within the bound.
No kernel may reach another device: no remote copies, remote signals or barrier semaphores. Data moves between devices by JAX's collectives and lax.ppermute only.
A program may use at most 64 MiB of HBM per device.

v0:
```python
import jax
import jax.numpy as jnp
from jax import lax
from jax.sharding import PartitionSpec as P

adapter_factor = 2.0


def selected_rows(value_entries, shard_portion, member_rows):
    shard_count = shard_portion.shape[0]
    adapter_rank = shard_portion.shape[1]
    flattened_rows = shard_portion.reshape(shard_count * adapter_rank, shard_portion.shape[2])
    rank_scores = lax.dot_general(
        value_entries, flattened_rows, (((1,), (1,)), ((), ())), preferred_element_type=jnp.float32
    )
    selected_entries = member_rows.astype(jnp.float32)
    return jnp.sum(
        rank_scores.reshape(value_entries.shape[0], shard_count, adapter_rank)
        * selected_entries[:, :, None],
        axis=1,
    )


def on_device(output_gradient, hidden, adapter_down, adapter_up, counts, offsets, adapter_slot):
    total_rows = output_gradient.shape[0]
    slots_per_worker = adapter_down.shape[0]
    adapter_rank = adapter_down.shape[1]
    hidden_size_count = hidden.shape[1]
    dp_count = lax.axis_size("dp")
    adapter_list = slots_per_worker * dp_count
    first_token = lax.axis_index("dp") * total_rows
    positions = first_token + lax.broadcasted_iota(jnp.int32, (total_rows, 1), 0)
    inside = (positions >= offsets[None, :]) & (positions < (offsets + counts)[None, :])
    slot_of_row = jnp.sum(jnp.where(inside, adapter_slot[None, :], 0), axis=1)
    columns = lax.broadcasted_iota(jnp.int32, (1, adapter_list), 1)
    member_rows = (slot_of_row[:, None] == columns).astype(jnp.bfloat16)
    up_portion = selected_rows(
        output_gradient, lax.all_gather(adapter_up, "dp", axis=0, tiled=True), member_rows
    )
    up_incoming = lax.psum(up_portion, "tensor").astype(jnp.bfloat16)
    broadcast_up = member_rows[:, :, None] * up_incoming[:, None, :]
    shard_portion = lax.all_gather(adapter_down, "dp", axis=0, tiled=True)
    shard_count = shard_portion.shape[0]
    flattened_rows = shard_portion.reshape(shard_count * adapter_rank, hidden_size_count)
    down_partial = selected_rows(hidden, shard_portion, member_rows)
    broadcast_portion = broadcast_up
    broadcast_portion = broadcast_portion.reshape(total_rows, shard_count * adapter_rank)
    gradient_running = jnp.dot(
        broadcast_portion, flattened_rows, preferred_element_type=jnp.float32
    )
    down_partial, gradient_running = (down_partial, gradient_running)
    down_incoming = lax.psum(down_partial, "tensor").astype(jnp.bfloat16)
    adapter_hidden_gradient = (adapter_factor * gradient_running).astype(jnp.bfloat16)
    broadcast_down = member_rows[:, :, None] * down_incoming[:, None, :]

    def slot_term(spread, value_entries, shard_count):
        broadcast_portion = spread
        broadcast_portion = broadcast_portion.reshape(total_rows, shard_count * adapter_rank)
        matrix_product = lax.dot_general(
            broadcast_portion,
            value_entries,
            (((0,), (0,)), ((), ())),
            preferred_element_type=jnp.float32,
        )
        return matrix_product.reshape(shard_count, adapter_rank, value_entries.shape[1])

    down_reduced = lax.psum_scatter(
        slot_term(broadcast_up, hidden, slots_per_worker * lax.axis_size("dp")).astype(
            jnp.bfloat16
        ),
        "dp",
        scatter_dimension=0,
        tiled=True,
    ).astype(jnp.float32)
    up_reduced = lax.psum_scatter(
        slot_term(broadcast_down, output_gradient, slots_per_worker * lax.axis_size("dp")).astype(
            jnp.bfloat16
        ),
        "dp",
        scatter_dimension=0,
        tiled=True,
    ).astype(jnp.float32)
    slot_grid = adapter_slot[:, None] == columns
    total_slots = jnp.sum(jnp.where(slot_grid, counts[:, None], 0), axis=0)
    scale_entries = adapter_factor / total_slots.astype(jnp.float32)
    owner_scale = lax.dynamic_slice_in_dim(
        scale_entries, lax.axis_index("dp") * slots_per_worker, slots_per_worker, 0
    )
    adapter_down_gradient = down_reduced * owner_scale[:, None, None]
    adapter_up_gradient = up_reduced * owner_scale[:, None, None]
    return (adapter_hidden_gradient, adapter_down_gradient, adapter_up_gradient)


def solution(mesh):
    placed = (
        P("dp", "tensor"),
        P("dp", "tensor"),
        P("dp", None, "tensor"),
        P("dp", None, "tensor"),
        P(),
        P(),
        P(),
    )
    return jax.shard_map(
        on_device,
        mesh=mesh,
        in_specs=placed,
        out_specs=(P("dp", "tensor"), P("dp", None, "tensor"), P("dp", None, "tensor")),
        check_vma=False,
    )
```

profile of v0, /device:TPU:2, one launch (start us, length us, event | category | flops | bytes accessed | tf_op | source)
XLA Modules:
  0.0 353.9 jit_solution(15384436137109650157)
XLA Ops:
  7.2 0.0 all-gather.3.cloned.1.call-start
  7.2 0.7 all-gather.3.cloned.1.call-update
  7.9 0.0 all-gather.5.cloned.1.call-start
  8.0 0.7 all-gather.5.cloned.1.call-update
  8.7 0.0 reduce-scatter.5.cloned.1.call-start
  8.7 0.7 add.27
  9.4 0.8 select_reduce_fusion
  10.2 51.6 %all-gather.3.cloned.1.call-done = bf16[64,16,1024]{2,1,0:T(8,128)(2,1)} async-done(((bf16[2,16,1024]{2,1,0:T(8,128)(2,1)}), bf16[64,16,1024]{2,1,0:T(8,128)(2,1)}) %all-gather.3.cloned.1.call-update) | async-done | bytes 2097168 | tf_op jit(solution)/shard_map/all_gather | solution.py:38
  61.8 4.2 %fusion.16 = f32[256,16]{0,1:T(8,128)S(1)} fusion(bf16[64,16,1024]{2,1,0:T(8,128)(2,1)} %all-gather.3.cloned.1.call-done, bf16[256,1024]{1,0:T(8,128)(2,1)} %param.7, f32[256,64]{0,1:T(8,128)S(1)} %get-tuple-element.6), kind=kOutput, calls=%fused_computation.13 | convolution fusion | flops 537391104 | bytes 2703360 | tf_op jit(solution)/shard_map/dot_general | solution.py:13
  66.0 53.4 %all-gather.5.cloned.1.call-done = bf16[64,16,3584]{2,1,0:T(8,128)(2,1)} async-done(((bf16[2,16,3584]{2,1,0:T(8,128)(2,1)}), bf16[64,16,3584]{2,1,0:T(8,128)(2,1)}) %all-gather.5.cloned.1.call-update) | async-done | bytes 7340048 | tf_op jit(solution)/shard_map/all_gather | solution.py:42
  119.4 11.0 %fusion.19 = f32[256,16]{0,1:T(8,128)S(1)} fusion(bf16[64,16,3584]{2,1,0:T(8,128)(2,1)} %all-gather.5.cloned.1.call-done, bf16[256,3584]{1,0:T(8,128)(2,1)S(1)} %copy-done, f32[256,64]{0,1:T(8,128)S(1)} %get-tuple-element.6), kind=kOutput, calls=%fused_computation.14 | convolution fusion | flops 1879568384 | bytes 9256960 | tf_op jit(solution)/shard_map/dot_general | solution.py:13
  130.3 30.3 %all-reduce = (bf16[256,16]{0,1:T(8,128)(2,1)S(1)}, bf16[256,16]{0,1:T(8,128)(2,1)S(1)}) all-reduce(f32[256,16]{0,1:T(8,128)S(1)} %fusion.16, f32[256,16]{0,1:T(8,128)S(1)} %fusion.19), channel_id=1, replica_groups=mesh['dp'=32,'tensor'=8] {'tensor'}, use_global_device_ids=true, to_apply=%region_2.3 | all-reduce | flops 8192 | bytes 49152 | tf_op jit(solution)/shard_map/psum | solution.py:40
  160.6 2.0 convolution_convert_fusion.1
  162.7 0.0 reduce-scatter.5.cloned.1.call-update
  162.7 0.0 reduce-scatter.3.cloned.1.call-start
  162.8 5.1 %convolution_convert_fusion = bf16[64,16,3584]{2,1,0:T(8,128)(2,1)} fusion(bf16[256,3584]{1,0:T(8,128)(2,1)S(1)} %copy-done, bf16[256,16]{0,1:T(8,128)(2,1)S(1)} %get-tuple-element.3, bf16[256,64]{0,1:T(8,128)(2,1)S(1)} %get-tuple-element.5), kind=kOutput, calls=%fused_computation | convolution fusion | flops 1882980352 | bytes 9216000 | tf_op jit(solution)/shard_map/dot_general | solution.py:59
  167.9 0.6 copy-done.2
  168.5 0.1 select_reduce_fusion.1
  168.6 0.1 dynamic_slice.3
  168.7 6.5 %fusion.3 = bf16[256,3584]{1,0:T(8,128)(2,1)} fusion(bf16[64,16,3584]{2,1,0:T(8,128)(2,1)} %all-gather.5.cloned.1.call-done, bf16[256,16]{0,1:T(8,128)(2,1)S(1)} %get-tuple-element.3, bf16[256,64]{0,1:T(8,128)(2,1)S(1)} %get-tuple-element.5), kind=kOutput, calls=%fused_computation.5 | convolution fusion | flops 1881145344 | bytes 9216000 | tf_op jit(solution)/shard_map/dot_general | solution.py:48
  175.2 70.9 %reduce-scatter.5.cloned.1.call-done = bf16[2,16,1024]{2,1,0:T(8,128)(2,1)} async-done(((bf16[64,16,1024]{2,1,0:T(8,128)(2,1)}), bf16[2,16,1024]{2,1,0:T(8,128)(2,1)}) %reduce-scatter.5.cloned.1.call-update) | async-done | bytes 65552 | tf_op jit(solution)/shard_map/reduce_scatter | solution.py:75
  246.1 1.6 convert_multiply_fusion.1
  247.7 97.9 %reduce-scatter.3.cloned.1.call-done = bf16[2,16,3584]{2,1,0:T(8,128)(2,1)} async-done(((bf16[64,16,3584]{2,1,0:T(8,128)(2,1)}), bf16[2,16,3584]{2,1,0:T(8,128)(2,1)}) %reduce-scatter.3.cloned.1.call-update) | async-done | bytes 229392 | tf_op jit(solution)/shard_map/reduce_scatter | solution.py:67
  345.6 1.8 convert_multiply_fusion
  (11 shorter events, 0.1 us)
Async XLA Ops:
  7.2 112.2 %copy-start = (bf16[256,3584]{1,0:T(8,128)(2,1)S(1)}, bf16[256,3584]{1,0:T(8,128)(2,1)}, u32[]{:S(2)}) copy-start(bf16[256,3584]{1,0:T(8,128)(2,1)} %param.8) | copy-start | bytes 5505028
  7.2 54.6 %all-gather.3.cloned.1.call-start = ((), (), s32[]{:S(2)}) async-start(), calls=%async_computation.2 | async-start | bytes 2162688 | tf_op jit(solution)/shard_map/all_gather | solution.py:38
  7.9 111.5 %all-gather.5.cloned.1.call-start = ((), (), s32[]{:S(2)}) async-start(), calls=%async_computation.3 | async-start | bytes 7569408 | tf_op jit(solution)/shard_map/all_gather | solution.py:42
  8.7 237.5 %reduce-scatter.5.cloned.1.call-start = ((), (), s32[]{:S(2)}) async-start(), calls=%async_computation.5 | async-start | bytes 2162688 | tf_op jit(solution)/shard_map/reduce_scatter | solution.py:75
  66.0 94.6 %copy-start.1 = (bf16[256,1024]{1,0:T(8,128)(2,1)S(1)}, bf16[256,1024]{1,0:T(8,128)(2,1)}, u32[]{:S(2)}) copy-start(bf16[256,1024]{1,0:T(8,128)(2,1)} %param.7) | copy-start | bytes 1572868
  162.7 182.9 %reduce-scatter.3.cloned.1.call-start = ((), (), s32[]{:S(2)}) async-start(), calls=%async_computation.4 | async-start | bytes 7569408 | tf_op jit(solution)/shard_map/reduce_scatter | solution.py:67
  167.9 0.7 copy-start.2
  167.9 0.7 copy-start.3
Sparse Core Ops, SparseCore 0:
  10.5 51.1 all-gather.2
  64.3 55.0 all-gather.4
  162.8 83.2 reduce-scatter.4
  250.0 95.5 reduce-scatter.2
where the time goes:
time: 354 us
  waiting for transfers between devices  275 us (78%)
  blocking collectives  30.3 us (9%)
  matrix products  28.8 us (8%)
  between operations  13.8 us (4%)
  other arithmetic  4.95 us (1%)
    reduce_scatter x1, waiting for transfers between devices, on_device(): lax.psum_scatter(slot_term(broadcast_up, hidden, slots_per_worker * lax.a...  97.9 us
    reduce_scatter x1, waiting for transfers between devices, on_device(): lax.psum_scatter(slot_term(broadcast_down, output_gradient, slots_per_wor...  70.9 us
    all_gather x1, waiting for transfers between devices, on_device(): shard_portion = lax.all_gather(adapter_down, 'dp', axis=0, tiled=True)  53.4 us
    all_gather x1, waiting for transfers between devices, on_device(): lax.all_gather(adapter_up, 'dp', axis=0, tiled=True)  51.6 us
    psum x1, blocking collectives, on_device(): up_incoming = lax.psum(up_portion, 'tensor').astype(jnp.bfloat16)  30.3 us
    dot_general x2, matrix products, selected_rows(): lax.dot_general(value_entries, flattened_rows, (((1,), (1,)), ((), ())),...  15.2 us
    dot_general x2, matrix products, slot_term(): lax.dot_general(broadcast_portion, value_entries, (((0,), (0,)), ((), ())...  7.15 us
  transfers between devices with their start and end apart: 4, of which 4 were waited for; matrix products, arithmetic and copies ran while one was open for 5% of the time, Pallas kernels for 0%

commit v1 on v0

--- a/solution.py
+++ b/solution.py
@@ -37,7 +37,7 @@
     up_portion = selected_rows(
         output_gradient, lax.all_gather(adapter_up, "dp", axis=0, tiled=True), member_rows
     )
-    up_incoming = lax.psum(up_portion, "tensor").astype(jnp.bfloat16)
+    up_incoming = jnp.sum(lax.all_gather(up_portion, "tensor"), axis=0).astype(jnp.bfloat16)
     broadcast_up = member_rows[:, :, None] * up_incoming[:, None, :]
     shard_portion = lax.all_gather(adapter_down, "dp", axis=0, tiled=True)
     shard_count = shard_portion.shape[0]

time: 354 us -> 317 us (0.90)
  waiting for transfers between devices: 275 us -> 212 us
  blocking collectives: 30.3 us -> 56.2 us
    reduce_scatter x1, waiting for transfers between devices: 97.9 us -> 49.9 us  [on_device(): lax.psum_scatter(slot_term(broadcast_up, hidden, slots_per_worker * lax.a...]
    all_gather x1, waiting for transfers between devices: 53.4 us -> 21.3 us  [on_device(): shard_portion = lax.all_gather(adapter_down, 'dp', axis=0, tiled=True)]
    all_gather x0 -> x1, blocking collectives: none -> 26 us  [on_device(): lax.all_gather(up_portion, 'tensor')]
    reduce_scatter x1, waiting for transfers between devices: 70.9 us -> 87.8 us  [on_device(): lax.psum_scatter(slot_term(broadcast_down, output_gradient, slots_per_wor...]
  transfers between devices with their start and end apart: 4 -> 4, of which waited for: 4 -> 4; matrix products, arithmetic and copies ran while one was open for 5% -> 10% of each run, Pallas kernels for 0% -> 0%
where the time goes in v1:
time: 317 us
  waiting for transfers between devices  212 us (67%)
  blocking collectives  56.2 us (18%)
  matrix products  28.8 us (9%)
  between operations  13.8 us (4%)
  other arithmetic  4.99 us (2%)
    reduce_scatter x1, waiting for transfers between devices, on_device(): lax.psum_scatter(slot_term(broadcast_down, output_gradient, slots_per_wor...  87.8 us
    all_gather x1, waiting for transfers between devices, on_device(): lax.all_gather(adapter_up, 'dp', axis=0, tiled=True)  51.6 us
    reduce_scatter x1, waiting for transfers between devices, on_device(): lax.psum_scatter(slot_term(broadcast_up, hidden, slots_per_worker * lax.a...  49.9 us
    psum x1, blocking collectives, on_device(): down_incoming = lax.psum(down_partial, 'tensor').astype(jnp.bfloat16)  30.2 us
    all_gather x1, blocking collectives, on_device(): lax.all_gather(up_portion, 'tensor')  26 us
    all_gather x1, waiting for transfers between devices, on_device(): shard_portion = lax.all_gather(adapter_down, 'dp', axis=0, tiled=True)  21.3 us
    dot_general x2, matrix products, selected_rows(): lax.dot_general(value_entries, flattened_rows, (((1,), (1,)), ((), ())),...  15.2 us
    dot_general x2, matrix products, slot_term(): lax.dot_general(broadcast_portion, value_entries, (((0,), (0,)), ((), ())...  7.15 us
  transfers between devices with their start and end apart: 4, of which 4 were waited for; matrix products, arithmetic and copies ran while one was open for 10% of the time, Pallas kernels for 0%

profile of v1, /device:TPU:2, one launch (start us, length us, event | category | flops | bytes accessed | tf_op | source)
XLA Modules:
  0.0 316.7 jit_solution(1351142453008852418)
XLA Ops:
  7.2 0.0 all-gather.4.cloned.1.call-start
  7.2 0.7 all-gather.4.cloned.1.call-update
  7.9 0.0 all-gather.6.cloned.1.call-start
  8.0 0.7 all-gather.6.cloned.1.call-update
  8.7 0.0 reduce-scatter.3.cloned.1.call-start
  8.7 0.7 add.25
  9.4 0.8 select_reduce_fusion
  10.2 51.6 %all-gather.4.cloned.1.call-done = bf16[64,16,1024]{2,1,0:T(8,128)(2,1)} async-done(((bf16[2,16,1024]{2,1,0:T(8,128)(2,1)}), bf16[64,16,1024]{2,1,0:T(8,128)(2,1)}) %all-gather.4.cloned.1.call-update) | async-done | bytes 2097168 | tf_op jit(solution)/shard_map/all_gather | solution.py:38
  61.8 4.2 %fusion.16 = f32[256,16]{0,1:T(8,128)S(1)} fusion(bf16[64,16,1024]{2,1,0:T(8,128)(2,1)} %all-gather.4.cloned.1.call-done, bf16[256,1024]{1,0:T(8,128)(2,1)} %param.7, f32[256,64]{0,1:T(8,128)S(1)} %get-tuple-element.4), kind=kOutput, calls=%fused_computation.13 | convolution fusion | flops 537391104 | bytes 2703360 | tf_op jit(solution)/shard_map/dot_general | solution.py:13
  66.0 26.0 %all-gather = f32[2048,16]{0,1:T(8,128)S(1)} all-gather(f32[256,16]{0,1:T(8,128)S(1)} %fusion.16), channel_id=2, replica_groups=mesh['dp'=32,'tensor'=8] {'tensor'}, dimensions={0}, use_global_device_ids=true | all-gather | bytes 147456 | tf_op jit(solution)/shard_map/all_gather | solution.py:40
  92.1 5.1 %convolution_convert_fusion = bf16[64,16,3584]{2,1,0:T(8,128)(2,1)} fusion(bf16[256,3584]{1,0:T(8,128)(2,1)S(1)} %copy-done, bf16[256,16]{0,1:T(8,128)(2,1)S(1)} %bitcast_reduce_fusion, bf16[256,64]{0,1:T(8,128)(2,1)S(1)} %get-tuple-element.3), kind=kOutput, calls=%fused_computation | convolution fusion | flops 1882980352 | bytes 9216000 | tf_op jit(solution)/shard_map/dot_general | solution.py:59
  97.3 0.2 reduce-scatter.5.cloned.1.call-start
  97.5 0.4 copy-done.2
  97.9 0.1 select_reduce_fusion.1
  98.0 0.1 dynamic_slice.3
  98.1 21.3 %all-gather.6.cloned.1.call-done = bf16[64,16,3584]{2,1,0:T(8,128)(2,1)} async-done(((bf16[2,16,3584]{2,1,0:T(8,128)(2,1)}), bf16[64,16,3584]{2,1,0:T(8,128)(2,1)}) %all-gather.6.cloned.1.call-update) | async-done | bytes 7340048 | tf_op jit(solution)/shard_map/all_gather | solution.py:42
  119.4 11.0 %fusion.19 = f32[256,16]{0,1:T(8,128)S(1)} fusion(bf16[64,16,3584]{2,1,0:T(8,128)(2,1)} %all-gather.6.cloned.1.call-done, bf16[256,3584]{1,0:T(8,128)(2,1)S(1)} %copy-done, f32[256,64]{0,1:T(8,128)S(1)} %get-tuple-element.4), kind=kOutput, calls=%fused_computation.14 | convolution fusion | flops 1879568384 | bytes 9256960 | tf_op jit(solution)/shard_map/dot_general | solution.py:13
  130.4 30.2 %psum.7 = bf16[256,16]{0,1:T(8,128)(2,1)S(1)} all-reduce(f32[256,16]{0,1:T(8,128)S(1)} %fusion.19), channel_id=1, replica_groups=mesh['dp'=32,'tensor'=8] {'tensor'}, use_global_device_ids=true, to_apply=%region_6.7 | all-reduce | flops 4096 | bytes 24576 | tf_op jit(solution)/shard_map/psum | solution.py:52
  160.6 2.0 convolution_convert_fusion.1
  162.6 6.4 %fusion.3 = bf16[256,3584]{1,0:T(8,128)(2,1)} fusion(bf16[64,16,3584]{2,1,0:T(8,128)(2,1)} %all-gather.6.cloned.1.call-done, bf16[256,16]{0,1:T(8,128)(2,1)S(1)} %bitcast_reduce_fusion, bf16[256,64]{0,1:T(8,128)(2,1)S(1)} %get-tuple-element.3), kind=kOutput, calls=%fused_computation.5 | convolution fusion | flops 1881145344 | bytes 9216000 | tf_op jit(solution)/shard_map/dot_general | solution.py:48
  169.1 49.9 %reduce-scatter.3.cloned.1.call-done = bf16[2,16,3584]{2,1,0:T(8,128)(2,1)} async-done(((bf16[64,16,3584]{2,1,0:T(8,128)(2,1)}), bf16[2,16,3584]{2,1,0:T(8,128)(2,1)}) %reduce-scatter.3.cloned.1.call-update) | async-done | bytes 229392 | tf_op jit(solution)/shard_map/reduce_scatter | solution.py:67
  219.0 1.8 convert_multiply_fusion
  220.8 87.8 %reduce-scatter.5.cloned.1.call-done = bf16[2,16,1024]{2,1,0:T(8,128)(2,1)} async-done(((bf16[64,16,1024]{2,1,0:T(8,128)(2,1)}), bf16[2,16,1024]{2,1,0:T(8,128)(2,1)}) %reduce-scatter.5.cloned.1.call-update) | async-done | bytes 65552 | tf_op jit(solution)/shard_map/reduce_scatter | solution.py:75
  308.6 1.6 convert_multiply_fusion.1
  (14 shorter events, 0.2 us)
Async XLA Ops:
  7.2 84.9 %copy-start = (bf16[256,3584]{1,0:T(8,128)(2,1)S(1)}, bf16[256,3584]{1,0:T(8,128)(2,1)}, u32[]{:S(2)}) copy-start(bf16[256,3584]{1,0:T(8,128)(2,1)} %param.8) | copy-start | bytes 5505028
  7.2 54.6 %all-gather.4.cloned.1.call-start = ((), (), s32[]{:S(2)}) async-start(), calls=%async_computation.2 | async-start | bytes 2162688 | tf_op jit(solution)/shard_map/all_gather | solution.py:38
  7.9 111.5 %all-gather.6.cloned.1.call-start = ((), (), s32[]{:S(2)}) async-start(), calls=%async_computation.3 | async-start | bytes 7569408 | tf_op jit(solution)/shard_map/all_gather | solution.py:42
  8.7 210.3 %reduce-scatter.3.cloned.1.call-start = ((), (), s32[]{:S(2)}) async-start(), calls=%async_computation.4 | async-start | bytes 7569408 | tf_op jit(solution)/shard_map/reduce_scatter | solution.py:67
  97.2 0.7 copy-start.2
  97.2 0.7 copy-start.3
  97.3 211.4 %reduce-scatter.5.cloned.1.call-start = ((), (), s32[]{:S(2)}) async-start(), calls=%async_computation.5 | async-start | bytes 2162688 | tf_op jit(solution)/shard_map/reduce_scatter | solution.py:75
  98.1 62.5 %copy-start.1 = (bf16[256,1024]{1,0:T(8,128)(2,1)S(1)}, bf16[256,1024]{1,0:T(8,128)(2,1)}, u32[]{:S(2)}) copy-start(bf16[256,1024]{1,0:T(8,128)(2,1)} %param.7) | copy-start | bytes 1572868
Sparse Core Ops, SparseCore 0:
  10.5 51.1 all-gather.3
  64.3 55.0 all-gather.5
  123.4 95.4 reduce-scatter.2
  222.7 85.9 reduce-scatter.4
